TPU v7x, 512 devices: a whole 4x8x8 slice. The times are simulated.
512 devices in a mesh: rows: 32 (over z, x), piv: 16 (over y, core).
Axes of the slice: x: 4, y: 8, z: 8, core: 2. Of those that a mesh axis runs over, the one named last changes fastest.
Arguments:
- ancestor_sol: float32 [1024, 32768], P('piv', 'rows'), may hold values from -6 to 6
- front_map: int32 [256], P('rows'), may hold values from 0 to 255, each once
- lower_panel: float32 [32768, 12288], P('rows', 'piv'), may hold values from -0.03125 to 0.03125
- inverse_factor: float32 [12288, 12288], P('piv', 'rows'), as said below
- right_side: float32 [1024, 12288], P(None, ('piv', 'rows')), may hold values from -6 to 6
- child_start: int32 [128], P('rows'), may hold values from 0 to 12287, as said below
- child_len: int32 [128], P('rows'), may hold values from 1 to 128, as said below
Outputs:
- child_blocks: float32 [1024, 16384], P('piv', 'rows')
Inputs may be any that keep to these rules, and one draw needn't show every extreme that they name: Child block c lies within pivots k * 384 to (k + 1) * 384 - 1, with k = c // 4; child_start[c] + child_len[c] <= (k + 1) * 384. `child_len`: child block 0 is full. inverse_factor is lower triangular with a diagonal in [0.5, 2].
All inputs are finite; a program needn't handle non-finite values.
Results may differ from a plain program's by a relative error of at most 0.000088.
Values sent between devices are 32-bit elements; how exact they have to be, the bound alone decides.
No kernel may reach another device: no remote copies, remote signals or barrier semaphores. Data moves between devices by JAX's collectives and lax.ppermute only.
A program may use at most 64 MiB of HBM per device.

v0:
```python
import jax
import jax.numpy as jnp
from jax import lax
from jax.sharding import Mesh
from jax.sharding import PartitionSpec as P

ROW_BLK = 128
CHILD_BLK = 128
ROWS = ("rows_0", "rows_1")
PIV_ROWS = ("piv", "rows_0", "rows_1")


def scatter_axes(value, axes, dim):
    if not axes:
        return value
    nearer = lax.psum_scatter(value, axes[0], scatter_dimension=dim, tiled=True)
    return scatter_axes(nearer, axes[1:], dim)


def gather_axes(value, axes, dim):
    for axis in reversed(axes):
        value = lax.all_gather(value, axis, axis=dim, tiled=True)
    return value


def in_blocks(value, dim, size):
    lengths = value.shape
    parts = value.reshape(*lengths[:dim], size, lengths[dim] // size, *lengths[dim + 1 :])
    return jnp.moveaxis(parts, dim, 0)


def sent_and_summed(value, axis, dim):
    parts = in_blocks(value, dim, lax.axis_size(axis))
    arrived = lax.all_to_all(parts, axis, split_axis=0, concat_axis=0, tiled=True)
    return arrived.sum(axis=0)


def body(ancestor_sol, front_map, lower_panel, inverse_factor, right_side, child_start, child_len):
    local_srcs = ancestor_sol.shape[0]
    count = front_map.shape[0]
    empty = jnp.zeros((local_srcs, count * ROW_BLK), jnp.float32)
    carry = empty
    piece = lax.all_gather(ancestor_sol, ROWS, axis=1, tiled=True)
    width = piece.shape[1]
    for block in range(count):
        offset = front_map[block] * ROW_BLK
        inside = (offset >= 0) & (offset < width)
        taken = lax.dynamic_slice_in_dim(piece, jnp.clip(offset, 0, width - ROW_BLK), ROW_BLK, 1)
        previous = carry[:, block * ROW_BLK : (block + 1) * ROW_BLK]
        carry = carry.at[:, block * ROW_BLK : (block + 1) * ROW_BLK].set(
            jnp.where(inside, taken, previous)
        )
    boundary = lax.all_gather(carry, "piv", axis=0, tiled=True)
    coupled = jnp.dot(
        boundary, lower_panel, precision=lax.Precision.HIGHEST, preferred_element_type=jnp.float32
    )
    span = inverse_factor.shape[1]
    share = right_side - scatter_axes(coupled, ROWS, 1)
    partial_sol = jnp.dot(
        gather_axes(share, ROWS, 1),
        inverse_factor,
        precision=lax.Precision.HIGHEST,
        preferred_element_type=jnp.float32,
    )
    slots = jnp.arange(CHILD_BLK, dtype=jnp.int32)
    local_first = child_start - lax.axis_index(ROWS) * span
    columns = jnp.clip(local_first[:, None] + slots[None, :], 0, span - 1).reshape(-1)
    valid = (slots[None, :] < child_len[:, None]).reshape(-1)[None, :]
    summed = sent_and_summed(partial_sol, "piv", 0)
    picked = jnp.take(summed, columns, axis=1)
    return jnp.where(valid, picked, jnp.zeros_like(picked))


def solution(mesh):
    torus = Mesh(mesh.devices.reshape(8, 4, mesh.shape["piv"]), ("rows_0", "rows_1", "piv"))
    return jax.shard_map(
        body,
        mesh=torus,
        in_specs=(
            P("piv", ROWS),
            P(ROWS),
            P(ROWS, "piv"),
            P("piv", ROWS),
            P(None, PIV_ROWS),
            P(ROWS),
            P(ROWS),
        ),
        out_specs=P("piv", ROWS),
        check_vma=False,
    )
```

profile of v0, /device:TPU:1, one launch (start us, length us, event | category | flops | bytes accessed | tf_op | source)
XLA Modules:
  0.0 392.0 jit_solution(8113103257739380664)
XLA Ops:
  6.5 0.7 all-gather.4.cloned.1.call-update
  7.3 0.0 all-gather.6.cloned.1.call-start
  7.3 1.6 fusion.7
  13.9 0.7 compare_reduce_fusion.6
  14.6 0.7 compare_reduce_fusion.5
  15.2 0.6 compare_reduce_fusion.4
  15.9 0.6 compare_reduce_fusion.3
  16.5 0.7 compare_reduce_fusion.2
  17.2 0.7 compare_reduce_fusion.1
  17.9 0.6 compare_reduce_fusion
  18.5 100.8 %all-gather.4.cloned.1.call-done = f32[64,32768]{1,0:T(8,128)} async-done(((f32[64,1024]{1,0:T(8,128)}), f32[64,32768]{1,0:T(8,128)}) %all-gather.4.cloned.1.call-update) | async-done | bytes 8388624 | tf_op jit(solution)/shard_map/all_gather | solution.py:43
  119.3 1.5 select_select_fusion.5
  120.9 1.6 select_dynamic-update-slice_fusion
  122.4 1.5 fusion
  123.9 1.5 fusion.1
  125.5 1.5 fusion.2
  127.0 1.5 fusion.3
  128.6 1.5 fusion.4
  130.1 0.9 fusion.5
  131.0 0.0 copy-start.1
  131.0 0.7 copy-done.1
  131.7 0.0 all-gather.6.cloned.1.call-update
  131.7 0.0 reduce-scatter.3.cloned.1.call-start
  131.8 42.2 %all-gather.6.cloned.1.call-done = f32[1024,1024]{1,0:T(8,128)} async-done(((f32[64,1024]{1,0:T(8,128)}), f32[1024,1024]{1,0:T(8,128)}) %all-gather.6.cloned.1.call-update) | async-done | bytes 4194320 | tf_op jit(solution)/shard_map/all_gather | solution.py:53
  174.0 13.0 %fusion.8 = f32[1024,768]{0,1:T(8,128)} fusion(f32[1024,1024]{1,0:T(8,128)} %all-gather.6.cloned.1.call-done, f32[1024,768]{1,0:T(8,128)S(1)} %copy-done), kind=kOutput, calls=%fused_computation.33 | convolution fusion | flops 9663676416 | bytes 10485760 | tf_op jit(solution)/shard_map/dot_general | solution.py:54
  187.0 0.0 reduce-scatter.3.cloned.1.call-update
  187.0 0.0 reduce-scatter.5.cloned.1.call-start
  187.1 45.9 %reduce-scatter.3.cloned.1.call-done = f32[1024,96]{0,1:T(8,128)} async-done(((f32[1024,768]{0,1:T(8,128)}), f32[1024,96]{0,1:T(8,128)}) %reduce-scatter.3.cloned.1.call-update) | async-done | bytes 393232 | tf_op jit(solution)/shard_map/reduce_scatter | solution.py:16
  232.9 0.0 reduce-scatter.5.cloned.1.call-update
  233.0 0.0 all-gather.8.cloned.1.call-start
  233.0 28.4 %reduce-scatter.5.cloned.1.call-done = f32[1024,24]{0,1:T(8,128)} async-done(((f32[1024,96]{0,1:T(8,128)}), f32[1024,24]{0,1:T(8,128)}) %reduce-scatter.5.cloned.1.call-update) | async-done | bytes 98320 | tf_op jit(solution)/shard_map/reduce_scatter | solution.py:16
  261.5 0.9 sub.11
  262.4 10.4 %all_gather.14 = f32[1024,96]{0,1:T(8,128)} all-gather(f32[1024,24]{0,1:T(8,128)S(1)} %sub.11), channel_id=1, replica_groups=mesh['rows_0'=8,'rows_1'=4,'piv'=16] {'rows_1'}, dimensions={1}, use_global_device_ids=true | all-gather | bytes 491520 | tf_op jit(solution)/shard_map/all_gather | solution.py:22
  272.7 0.0 all-gather.8.cloned.1.call-update
  272.8 0.0 copy-start.3
  272.8 0.0 copy-start.4
  272.8 53.3 %all-gather.8.cloned.1.call-done = f32[1024,768]{0,1:T(8,128)} async-done(((f32[1024,96]{0,1:T(8,128)}), f32[1024,768]{0,1:T(8,128)}) %all-gather.8.cloned.1.call-update) | async-done | bytes 3145744 | tf_op jit(solution)/shard_map/all_gather | solution.py:22
  326.1 7.9 %fusion.9 = f32[1024,384]{1,0:T(8,128)} fusion(f32[1024,768]{0,1:T(8,128)} %all-gather.8.cloned.1.call-done, f32[768,384]{1,0:T(8,128)} %param.26), kind=kOutput, calls=%fused_computation.34 | convolution fusion | flops 3623878656 | bytes 5898240 | tf_op jit(solution)/shard_map/dot_general | solution.py:59
  334.0 7.6 %all-to-all-start = ((f32[16,64,384]{2,1,0:T(8,128)}), f32[16,64,384]{2,1,0:T(8,128)}, u32[]{:S(2)}, u32[]{:S(2)}) async-start(f32[16,64,384]{2,1,0:T(8,128)} %bitcast.31), calls=%async_computation.2 | async-start | bytes 3145728 | tf_op jit(solution)/shard_map/all_to_all | solution.py:34
  341.6 0.1 add_clamp_fusion
  341.7 0.1 compare_and_fusion
  341.8 0.1 fusion.6
  341.9 38.4 %all-to-all-done = f32[16,64,384]{2,1,0:T(8,128)} async-done(((f32[16,64,384]{2,1,0:T(8,128)}), f32[16,64,384]{2,1,0:T(8,128)}, u32[]{:S(2)}, u32[]{:S(2)}) %all-to-all-start) | async-done | bytes 1572896 | tf_op jit(solution)/shard_map/all_to_all | solution.py:34
  380.2 1.5 reduce_sum.9
  381.7 0.1 copy.9
  381.9 1.6 gather_fusion
  383.5 1.1 select_bitcast_fusion
  384.7 0.8 copy.10
  (11 shorter events, 0.1 us)
Async XLA Ops:
  6.5 167.4 %copy-start = (f32[1024,768]{1,0:T(8,128)S(1)}, f32[1024,768]{1,0:T(8,128)}, u32[]{:S(2)}) copy-start(f32[1024,768]{1,0:T(8,128)} %param.25) | copy-start | bytes 9437188
  6.5 112.8 %all-gather.4.cloned.1.call-start = ((), (), s32[]{:S(2)}) async-start(), calls=%async_computation.3 | async-start | bytes 8650752 | tf_op jit(solution)/shard_map/all_gather | solution.py:43
  7.3 166.7 %all-gather.6.cloned.1.call-start = ((), (), s32[]{:S(2)}) async-start(), calls=%async_computation.4 | async-start | bytes 4456448 | tf_op jit(solution)/shard_map/all_gather | solution.py:53
  131.0 0.7 copy-start.1
  131.7 101.2 %reduce-scatter.3.cloned.1.call-start = ((), (), s32[]{:S(2)}) async-start(), calls=%async_computation.5 | async-start | bytes 3538944 | tf_op jit(solution)/shard_map/reduce_scatter | solution.py:16
  187.0 74.5 %copy-start.2 = (f32[1024,24]{0,1:T(8,128)S(1)}, f32[1024,24]{0,1:T(8,128)}, u32[]{:S(2)}) copy-start(f32[1024,24]{0,1:T(8,128)} %param.27) | copy-start | bytes 294916
  187.0 74.4 %reduce-scatter.5.cloned.1.call-start = ((), (), s32[]{:S(2)}) async-start(), calls=%async_computation.6 | async-start | bytes 491520 | tf_op jit(solution)/shard_map/reduce_scatter | solution.py:16
  233.0 93.1 %all-gather.8.cloned.1.call-start = ((), (), s32[]{:S(2)}) async-start(), calls=%async_computation.7 | async-start | bytes 3538944 | tf_op jit(solution)/shard_map/all_gather | solution.py:22
  272.8 68.8 %copy-start.3 = (s32[4]{0:T(128)S(1)}, s32[4]{0:T(128)}, u32[]{:S(2)}) copy-start(s32[4]{0:T(128)} %param.28) | copy-start | bytes 52
  272.8 69.0 %copy-start.4 = (s32[4]{0:T(128)S(1)}, s32[4]{0:T(128)}, u32[]{:S(2)}) copy-start(s32[4]{0:T(128)} %param.29) | copy-start | bytes 52
  334.0 46.2 %all-to-all-start = ((f32[16,64,384]{2,1,0:T(8,128)}), f32[16,64,384]{2,1,0:T(8,128)}, u32[]{:S(2)}, u32[]{:S(2)}) async-start(f32[16,64,384]{2,1,0:T(8,128)} %bitcast.31), calls=%async_computation.2 | async-start | bytes 3145728 | tf_op jit(solution)/shard_map/all_to_all | solution.py:34
Sparse Core Ops, SparseCore 0:
  10.5 108.7 all-gather.3
  131.8 42.0 all-gather.5
  187.1 45.7 reduce-scatter.2
  235.6 25.7 reduce-scatter.4
  272.9 53.1 all-gather.7
where the time goes:
time: 393 us; the launch traced here: 392 us
  waiting for transfers between devices  310 us (79%)
  matrix products  21 us (5%)
  other arithmetic  20 us (5%)
  between operations  18.2 us (5%)
  blocking collectives  10.4 us (3%)
  starting transfers between devices  7.75 us (2%)
  local copies, waits for them, and re-layouts  4.88 us (1%)
    all_gather x1, waiting for transfers between devices, body(): piece = lax.all_gather(ancestor_sol, ROWS, axis=1, tiled=True)  101 us
    reduce_scatter x2, waiting for transfers between devices, scatter_axes(): nearer = lax.psum_scatter(value, axes[0], scatter_dimension=dim, tiled=True)  74.3 us
    all_gather x1, waiting for transfers between devices, gather_axes(): value = lax.all_gather(value, axis, axis=dim, tiled=True)  53.3 us
    all_gather x1, waiting for transfers between devices, body(): boundary = lax.all_gather(carry, 'piv', axis=0, tiled=True)  42.2 us
    all_to_all x1, waiting for transfers between devices, sent_and_summed(): lax.all_to_all(parts, axis, split_axis=0, concat_axis=0, tiled=True)  38.4 us
    dot_general x1, matrix products, body(): jnp.dot(boundary, lower_panel, precision=lax.Precision.HIGHEST, preferred...  13 us
    all_gather x1, blocking collectives, gather_axes(): value = lax.all_gather(value, axis, axis=dim, tiled=True)  10.4 us
    scatter x7, other arithmetic, body(): carry.at[:, block * ROW_BLK:(block + 1) * ROW_BLK]  10.1 us
  transfers between devices with their start and end apart: 6, of which 6 were waited for; matrix products, arithmetic and copies ran while one was open for 2% of the time, Pallas kernels for 0%

commit v1 on v0

--- a/solution.py
+++ b/solution.py
@@ -40,7 +40,10 @@
     count = front_map.shape[0]
     empty = jnp.zeros((local_srcs, count * ROW_BLK), jnp.float32)
     carry = empty
-    piece = lax.all_gather(ancestor_sol, ROWS, axis=1, tiled=True)
+    n_dev = lax.axis_size(ROWS)
+    blocks = jnp.stack([ancestor_sol for _ in range(n_dev)])
+    blocks = lax.all_to_all(blocks, ROWS, split_axis=0, concat_axis=0)
+    piece = jnp.concatenate(blocks, axis=1)
     width = piece.shape[1]
     for block in range(count):
         offset = front_map[block] * ROW_BLK

time: 393 us -> 495 us (1.26)
  waiting for transfers between devices: 310 us -> 396 us
  starting transfers between devices: 7.75 us -> 21.7 us
  local copies, waits for them, and re-layouts: 4.88 us -> 13.6 us
  other arithmetic: 20 us -> 13.5 us
    all_to_all x0 -> x1, waiting for transfers between devices: none -> 177 us  [body(): blocks = lax.all_to_all(blocks, ROWS, split_axis=0, concat_axis=0)]
    all_gather x1 -> x0, waiting for transfers between devices: 101 us -> none  [body(): piece = lax.all_gather(ancestor_sol, ROWS, axis=1, tiled=True)]
    all_to_all x0 -> x1, starting transfers between devices: none -> 14 us  [body(): blocks = lax.all_to_all(blocks, ROWS, split_axis=0, concat_axis=0)]
    all_gather x1, waiting for transfers between devices: 42.2 us -> 52.1 us  [body(): boundary = lax.all_gather(carry, 'piv', axis=0, tiled=True)]
    scatter x7, other arithmetic: 10.1 us -> 4.26 us  [body(): carry.at[:, block * ROW_BLK:(block + 1) * ROW_BLK]]
    another operation x0 -> x1, local copies, waits for them, and re-layouts: none -> 5.37 us  [body(): blocks = jnp.stack([ancestor_sol for _ in range(n_dev)])]
  transfers between devices with their start and end apart: 6 -> 6, of which waited for: 6 -> 6; matrix products, arithmetic and copies ran while one was open for 2% -> 1% of each run, Pallas kernels for 0% -> 0%
where the time goes in v1:
time: 495 us; the launch traced here: 494 us
  waiting for transfers between devices  396 us (80%)
  starting transfers between devices  21.7 us (4%)
  matrix products  21 us (4%)
  between operations  18.4 us (4%)
  local copies, waits for them, and re-layouts  13.6 us (3%)
  other arithmetic  13.5 us (3%)
  blocking collectives  10.4 us (2%)
    all_to_all x1, waiting for transfers between devices, body(): blocks = lax.all_to_all(blocks, ROWS, split_axis=0, concat_axis=0)  177 us
    reduce_scatter x2, waiting for transfers between devices, scatter_axes(): nearer = lax.psum_scatter(value, axes[0], scatter_dimension=dim, tiled=True)  74.5 us
    all_gather x1, waiting for transfers between devices, gather_axes(): value = lax.all_gather(value, axis, axis=dim, tiled=True)  53.4 us
    all_gather x1, waiting for transfers between devices, body(): boundary = lax.all_gather(carry, 'piv', axis=0, tiled=True)  52.1 us
    all_to_all x1, waiting for transfers between devices, sent_and_summed(): lax.all_to_all(parts, axis, split_axis=0, concat_axis=0, tiled=True)  38.4 us
    all_to_all x1, starting transfers between devices, body(): blocks = lax.all_to_all(blocks, ROWS, split_axis=0, concat_axis=0)  14 us
    dot_general x1, matrix products, body(): jnp.dot(boundary, lower_panel, precision=lax.Precision.HIGHEST, preferred...  13 us
    all_gather x1, blocking collectives, gather_axes(): value = lax.all_gather(value, axis, axis=dim, tiled=True)  10.4 us
  transfers between devices with their start and end apart: 6, of which 6 were waited for; matrix products, arithmetic and copies ran while one was open for 1% of the time, Pallas kernels for 0%

profile of v1, /device:TPU:1, one launch (start us, length us, event | category | flops | bytes accessed | tf_op | source)
XLA Modules:
  0.0 494.1 jit_solution(4170344471010785743)
XLA Ops:
  6.5 5.4 %stack.2 = f32[32,64,1024]{2,1,0:T(8,128)} broadcast(f32[64,1024]{1,0:T(8,128)} %param.23), dimensions={1,2} | broadcast | bytes 8650752 | tf_op jit(solution)/shard_map/stack | solution.py:44
  11.9 14.0 %all-to-all-start = ((f32[32,64,1024]{2,1,0:T(8,128)}), f32[32,64,1024]{2,1,0:T(8,128)}, u32[]{:S(2)}, u32[]{:S(2)}) async-start(f32[32,64,1024]{2,1,0:T(8,128)} %stack.2), calls=%async_computation | async-start | bytes 16777216 | tf_op jit(solution)/shard_map/all_to_all | solution.py:45
  25.9 0.0 all-gather.3.cloned.1.call-start
  25.9 0.7 fusion.7
  31.8 0.7 compare_reduce_fusion.6
  32.5 0.6 compare_reduce_fusion.5
  33.1 0.6 compare_reduce_fusion.4
  33.7 0.7 compare_reduce_fusion.3
  34.4 0.7 compare_reduce_fusion.2
  35.1 0.7 compare_reduce_fusion.1
  35.8 0.7 compare_reduce_fusion
  36.4 177.1 %all-to-all-done = f32[32,64,1024]{2,1,0:T(8,128)} async-done(((f32[32,64,1024]{2,1,0:T(8,128)}), f32[32,64,1024]{2,1,0:T(8,128)}, u32[]{:S(2)}, u32[]{:S(2)}) %all-to-all-start) | async-done | bytes 8388640 | tf_op jit(solution)/shard_map/all_to_all | solution.py:45
  213.6 4.2 copy.14
  217.8 0.8 select_select_fusion.5
  218.6 0.6 select_dynamic-update-slice_fusion
  219.2 0.6 fusion
  219.9 0.8 fusion.1
  220.6 0.7 fusion.2
  221.4 0.7 fusion.3
  222.1 0.7 fusion.4
  222.8 0.1 fusion.5
  222.9 0.7 copy-done.1
  223.6 0.0 all-gather.3.cloned.1.call-update
  223.6 0.0 reduce-scatter.3.cloned.1.call-start
  223.6 52.1 %all-gather.3.cloned.1.call-done = f32[1024,1024]{1,0:T(8,128)} async-done(((f32[64,1024]{1,0:T(8,128)}), f32[1024,1024]{1,0:T(8,128)}) %all-gather.3.cloned.1.call-update) | async-done | bytes 4194320 | tf_op jit(solution)/shard_map/all_gather | solution.py:56
  275.8 13.0 %fusion.8 = f32[1024,768]{0,1:T(8,128)} fusion(f32[1024,1024]{1,0:T(8,128)} %all-gather.3.cloned.1.call-done, f32[1024,768]{1,0:T(8,128)S(1)} %copy-done), kind=kOutput, calls=%fused_computation.33 | convolution fusion | flops 9663676416 | bytes 10485760 | tf_op jit(solution)/shard_map/dot_general | solution.py:57
  288.8 0.0 reduce-scatter.3.cloned.1.call-update
  288.8 0.0 reduce-scatter.5.cloned.1.call-start
  288.9 45.9 %reduce-scatter.3.cloned.1.call-done = f32[1024,96]{0,1:T(8,128)} async-done(((f32[1024,768]{0,1:T(8,128)}), f32[1024,96]{0,1:T(8,128)}) %reduce-scatter.3.cloned.1.call-update) | async-done | bytes 393232 | tf_op jit(solution)/shard_map/reduce_scatter | solution.py:16
  334.8 0.0 reduce-scatter.5.cloned.1.call-update
  334.9 0.0 all-gather.5.cloned.1.call-start
  334.9 28.5 %reduce-scatter.5.cloned.1.call-done = f32[1024,24]{0,1:T(8,128)} async-done(((f32[1024,96]{0,1:T(8,128)}), f32[1024,24]{0,1:T(8,128)}) %reduce-scatter.5.cloned.1.call-update) | async-done | bytes 98320 | tf_op jit(solution)/shard_map/reduce_scatter | solution.py:16
  363.4 0.9 sub.11
  364.4 10.4 %all_gather.10 = f32[1024,96]{0,1:T(8,128)} all-gather(f32[1024,24]{0,1:T(8,128)S(1)} %sub.11), channel_id=1, replica_groups=mesh['rows_0'=8,'rows_1'=4,'piv'=16] {'rows_1'}, dimensions={1}, use_global_device_ids=true | all-gather | bytes 491520 | tf_op jit(solution)/shard_map/all_gather | solution.py:22
  374.7 0.0 all-gather.5.cloned.1.call-update
  374.7 0.0 copy-start.4
  374.8 53.4 %all-gather.5.cloned.1.call-done = f32[1024,768]{0,1:T(8,128)} async-done(((f32[1024,96]{0,1:T(8,128)}), f32[1024,768]{0,1:T(8,128)}) %all-gather.5.cloned.1.call-update) | async-done | bytes 3145744 | tf_op jit(solution)/shard_map/all_gather | solution.py:22
  428.2 7.9 %fusion.9 = f32[1024,384]{1,0:T(8,128)} fusion(f32[1024,768]{0,1:T(8,128)} %all-gather.5.cloned.1.call-done, f32[768,384]{1,0:T(8,128)} %param.26), kind=kOutput, calls=%fused_computation.34 | convolution fusion | flops 3623878656 | bytes 5898240 | tf_op jit(solution)/shard_map/dot_general | solution.py:62
  436.1 7.6 %all-to-all-start.1 = ((f32[16,64,384]{2,1,0:T(8,128)}), f32[16,64,384]{2,1,0:T(8,128)}, u32[]{:S(2)}, u32[]{:S(2)}) async-start(f32[16,64,384]{2,1,0:T(8,128)} %bitcast.42), calls=%async_computation.3 | async-start | bytes 3145728 | tf_op jit(solution)/shard_map/all_to_all | solution.py:34
  443.7 0.1 add_clamp_fusion
  443.8 0.1 compare_and_fusion
  443.9 0.1 fusion.6
  444.0 38.4 %all-to-all-done.1 = f32[16,64,384]{2,1,0:T(8,128)} async-done(((f32[16,64,384]{2,1,0:T(8,128)}), f32[16,64,384]{2,1,0:T(8,128)}, u32[]{:S(2)}, u32[]{:S(2)}) %all-to-all-start.1) | async-done | bytes 1572896 | tf_op jit(solution)/shard_map/all_to_all | solution.py:34
  482.4 1.5 reduce_sum.9
  483.9 0.1 copy.12
  484.0 1.6 gather_fusion
  485.6 1.1 select_bitcast_fusion
  486.8 0.8 copy.13
  (14 shorter events, 0.1 us)
Async XLA Ops:
  6.5 269.2 %copy-start = (f32[1024,768]{1,0:T(8,128)S(1)}, f32[1024,768]{1,0:T(8,128)}, u32[]{:S(2)}) copy-start(f32[1024,768]{1,0:T(8,128)} %param.25) | copy-start | bytes 9437188
  11.9 14.0 %copy-start.3 = (s32[8]{0:T(128)S(1)}, s32[8]{0:T(128)}, u32[]{:S(2)}) copy-start(s32[8]{0:T(128)} %param.24) | copy-start | bytes 100
  11.9 201.7 %all-to-all-start = ((f32[32,64,1024]{2,1,0:T(8,128)}), f32[32,64,1024]{2,1,0:T(8,128)}, u32[]{:S(2)}, u32[]{:S(2)}) async-start(f32[32,64,1024]{2,1,0:T(8,128)} %stack.2), calls=%async_computation | async-start | bytes 16777216 | tf_op jit(solution)/shard_map/all_to_all | solution.py:45
  25.9 249.9 %all-gather.3.cloned.1.call-start = ((), (), s32[]{:S(2)}) async-start(), calls=%async_computation.4 | async-start | bytes 4456448 | tf_op jit(solution)/shard_map/all_gather | solution.py:56
  222.9 0.7 copy-start.1
  223.6 111.2 %reduce-scatter.3.cloned.1.call-start = ((), (), s32[]{:S(2)}) async-start(), calls=%async_computation.5 | async-start | bytes 3538944 | tf_op jit(solution)/shard_map/reduce_scatter | solution.py:16
  288.8 74.6 %copy-start.2 = (f32[1024,24]{0,1:T(8,128)S(1)}, f32[1024,24]{0,1:T(8,128)}, u32[]{:S(2)}) copy-start(f32[1024,24]{0,1:T(8,128)} %param.27) | copy-start | bytes 294916
  288.8 74.6 %reduce-scatter.5.cloned.1.call-start = ((), (), s32[]{:S(2)}) async-start(), calls=%async_computation.6 | async-start | bytes 491520 | tf_op jit(solution)/shard_map/reduce_scatter | solution.py:16
  334.9 93.4 %all-gather.5.cloned.1.call-start = ((), (), s32[]{:S(2)}) async-start(), calls=%async_computation.7 | async-start | bytes 3538944 | tf_op jit(solution)/shard_map/all_gather | solution.py:22
  374.7 69.0 %copy-start.4 = (s32[4]{0:T(128)S(1)}, s32[4]{0:T(128)}, u32[]{:S(2)}) copy-start(s32[4]{0:T(128)} %param.28) | copy-start | bytes 52
  374.8 69.2 %copy-start.5 = (s32[4]{0:T(128)S(1)}, s32[4]{0:T(128)}, u32[]{:S(2)}) copy-start(s32[4]{0:T(128)} %param.29) | copy-start | bytes 52
  436.1 46.2 %all-to-all-start.1 = ((f32[16,64,384]{2,1,0:T(8,128)}), f32[16,64,384]{2,1,0:T(8,128)}, u32[]{:S(2)}, u32[]{:S(2)}) async-start(f32[16,64,384]{2,1,0:T(8,128)} %bitcast.42), calls=%async_computation.3 | async-start | bytes 3145728 | tf_op jit(solution)/shard_map/all_to_all | solution.py:34
Sparse Core Ops, SparseCore 0:
  223.7 52.0 all-gather.2
  289.0 45.8 reduce-scatter.2
  337.7 25.7 reduce-scatter.4
  374.9 53.2 all-gather.4
